TPU v7x, 128 devices: a whole 4x4x4 slice. The times are simulated.
128 devices in a mesh: sx: 8 (over y, core), sy: 16 (over x, z).
Axes of the slice: x: 4, y: 4, z: 4, core: 2. Of those that a mesh axis runs over, the one named last changes fastest.
Arguments:
- loads: float32 [8, 16, 1536, 256], P('sx', 'sy')
- schur_flex: float32 [8, 16, 1536, 1536], P('sx', 'sy'), as said below
- dirichlet: float32 [8, 16, 1536, 1536], P('sx', 'sy'), as said below
- coupling: float32 [8, 16, 16, 1536], P('sx', 'sy'), may hold values from -0.3125 to 0.3125
- corner_index: int32 [8, 16, 16], P('sx', 'sy'), may hold values from 0 to 512, as said below
- face_lists: int32 [8, 16, 4, 384], P('sx', 'sy'), may hold values from 0 to 383, as said below
- coarse_inverse: float32 [512, 512], P(('sx', 'sy')), as said below
Outputs:
- multipliers: float32 [8, 16, 1536, 256], P('sx', 'sy')
- residual: float32 [8, 16, 1536, 256], P('sx', 'sy')
Inputs may be any that keep to these rules, and one draw needn't show every extreme that they name: `corner_index`: each subdomain lists 4 coarse dofs for each of its four corners; 512 marks a corner on the clamped edges of the panel, which has no coarse dof; every coarse dof below 512 is named by some subdomain. `face_lists`: each face's list is a permutation of the 384 dofs of the facing face; the facing lists of two neighbouring subdomains are inverse permutations. `schur_flex`: symmetric positive definite for every subdomain. `dirichlet`: symmetric positive definite for every subdomain. `coarse_inverse`: symmetric positive definite.
All inputs are finite; a program needn't handle non-finite values.
Results may differ from a plain program's by a relative error of at most 0.00017.
Values sent between devices are 32-bit elements; how exact they have to be, the bound alone decides.
A program may use at most 128 MiB of HBM per device.

v0:
```python
import jax
import jax.numpy as jnp
from jax import lax
from jax.sharding import PartitionSpec as P

ITERS = 2


def shifted(block, axis, distance):
    devices = range(lax.axis_size(axis))
    route = [(i - distance, i) for i in devices if i - distance in devices]
    return lax.ppermute(block, axis, route)


def jump(field, face_index):
    size = field.shape[0] // 4
    width = field.shape[1]
    face_rows = field.reshape(4, size, width)
    from_low_x = shifted(face_rows[1], "sx", 1)
    from_high_x = shifted(face_rows[0], "sx", -1)
    from_low_y = shifted(face_rows[3], "sy", 1)
    from_high_y = shifted(face_rows[2], "sy", -1)
    received = jnp.stack([from_low_x, from_high_x, from_low_y, from_high_y], axis=0)
    matched = received[jnp.arange(4, dtype=jnp.int32)[:, None], face_index]
    return (face_rows - matched).reshape(4 * size, width)


def coarse_solve(coarse_rhs, stiffness_inverse_lines):
    highest = lax.Precision.HIGHEST
    total = lax.psum(coarse_rhs, ("sx", "sy"))
    mine = jnp.dot(stiffness_inverse_lines, total, precision=highest)
    return lax.all_gather(mine, ("sx", "sy"), axis=0, tiled=True)


def inner(first, second):
    return jnp.sum(first * second, axis=0)


def shards(loads, schur_flex, dirichlet, coupling, corner_index, face_lists, coarse_inverse):
    high = lax.Precision.HIGH
    highest = lax.Precision.HIGHEST
    flex_mat = schur_flex[0, 0]
    prec_mat = dirichlet[0, 0]
    coupling_mat = coupling[0, 0]
    corners = corner_index[0, 0]
    face_index = face_lists[0, 0]
    ncoarse = coarse_inverse.shape[1]
    onehot = (corners[None, :] == jnp.arange(ncoarse, dtype=jnp.int32)[:, None]).astype(jnp.float32)
    size = face_index.shape[1]
    sx = lax.axis_index("sx")
    sy = lax.axis_index("sy")
    inside = jnp.stack([sx > 0, sx < lax.axis_size("sx") - 1, sy > 0, sy < lax.axis_size("sy") - 1])
    scale = jnp.repeat(1.0 + inside.astype(jnp.float32), size)[:, None]

    def total(values):
        return lax.psum(values, ("sx", "sy"))

    residual = jump(loads[0, 0], face_index)
    multipliers = jnp.zeros_like(residual)
    direction = None
    residual_inner = None
    for iteration in range(ITERS):
        spread = scale * residual
        operator_applied = jnp.dot(prec_mat, spread, precision=high)
        new_dot = total(0.5 * inner(spread, operator_applied))
        precond = 0.5 * jump(operator_applied, face_index)
        direction = precond if iteration == 0 else precond + new_dot / residual_inner * direction
        residual_inner = new_dot
        apply_spread = scale * direction
        fine_part = jnp.dot(flex_mat, apply_spread, precision=high)
        local_load = jnp.dot(coupling_mat, apply_spread, precision=high)
        coarse_rhs = jnp.dot(onehot, local_load, precision=highest)
        coarse_sol = coarse_solve(coarse_rhs, coarse_inverse)
        filled_out = jnp.concatenate(
            [coarse_sol, jnp.zeros((1, direction.shape[1]), jnp.float32)], axis=0
        )
        picked = filled_out[corners]
        correction = lax.dot_general(coupling_mat, picked, (((0,), (0,)), ((), ())), precision=high)
        applied = fine_part + correction
        step_size = residual_inner / total(inner(apply_spread, applied))
        image_dir = jump(applied, face_index)
        multipliers = multipliers + step_size * direction
        residual = residual - step_size * image_dir
    return (multipliers[None, None], residual[None, None])


def solution(mesh):
    return jax.shard_map(
        shards,
        mesh=mesh,
        in_specs=(
            P("sx", "sy", None, None),
            P("sx", "sy", None, None),
            P("sx", "sy", None, None),
            P("sx", "sy", None, None),
            P("sx", "sy", None),
            P("sx", "sy", None, None),
            P(("sx", "sy"), None),
        ),
        out_specs=(P("sx", "sy", None, None), P("sx", "sy", None, None)),
        check_vma=False,
    )
```

profile of v0, /device:TPU:1, one launch (start us, length us, event | category | flops | bytes accessed | tf_op | source)
XLA Modules:
  0.0 859.2 jit_solution(2950131900494569318)
XLA Ops:
  10.0 5.0 collective-permute-start.2
  27.9 10.7 %gather_fusion = f32[1536,256]{1,0:T(8,128)S(1)} fusion(f32[4,384,256]{2,1,0:T(8,128)S(1)} %pad_maximum_fusion, s32[1536]{0:T(1024)S(1)} %reshape.131), kind=kCustom, calls=%fused_computation | custom fusion | bytes 3158016 | tf_op jit(solution)/shard_map/gather | solution.py:24
  38.6 11.8 %fusion.10 = f32[1536,256]{0,1:T(8,128)S(1)} fusion(f32[1,1,1536,1536]{3,2,1,0:T(8,128)} %param.9, f32[1,1,1536,256]{3,2,1,0:T(8,128)} %param.7, f32[1536,256]{1,0:T(8,128)S(1)} %gather_fusion, f32[1536]{0:T(1024)S(1)} %mul.105), kind=kOutput, calls=%fused_computation.19 | convolution fusion | flops 3624665088 | bytes 14161920 | tf_op jit(solution)/shard_map/dot_general | solution.py:64
  53.4 4.9 collective-permute-start.6
  60.2 4.8 collective-permute-start.4
  74.5 17.9 %gather_fusion.1 = f32[1536,256]{1,0:T(8,128)} fusion(f32[4,384,256]{2,1,0:T(8,128)S(1)} %copy.21, s32[1536]{0:T(1024)S(1)} %reshape.131), kind=kCustom, calls=%fused_computation.1 | custom fusion | bytes 3158016 | tf_op jit(solution)/shard_map/gather | solution.py:24
  100.6 6.7 fusion.2
  107.4 144.9 %all-reduce.6.cloned.1.call-done = f32[512,256]{1,0:T(8,128)} async-done(((f32[512,256]{1,0:T(8,128)}), f32[512,256]{1,0:T(8,128)}) %all-reduce.6.cloned.1.call-update) | async-done | bytes 524304 | tf_op jit(solution)/shard_map/psum | solution.py:30
  253.7 54.1 %all-gather = f32[128,4,256]{2,1,0:T(4,128)} all-gather(f32[1,4,256]{2,1,0:T(4,128)S(1)} %convolution_bitcast_fusion.1), channel_id=1, replica_groups=mesh['sx'=8,'sy'=16] {'sx','sy'}, dimensions={0}, use_global_device_ids=true | all-gather | bytes 528384 | tf_op jit(solution)/shard_map/all_gather | solution.py:32
  317.2 4.0 collective-permute-start.10
  326.8 64.9 %all-reduce.2 = (f32[256]{0:T(256)S(1)}, f32[256]{0:T(256)S(1)}) all-reduce(f32[256]{0:T(256)S(1)} %broadcast_multiply_fusion.3, f32[256]{0:T(256)S(1)} %get-tuple-element.34), channel_id=1, replica_groups=mesh['sx'=8,'sy'=16] {'sx','sy'}, use_global_device_ids=true, to_apply=%region_1.0 | all-reduce | flops 512 | bytes 4096 | tf_op jit(solution)/shard_map/psum | solution.py:56
  396.0 17.9 %gather_fusion.3 = f32[1536,256]{1,0:T(8,128)} fusion(f32[4,384,256]{2,1,0:T(8,128)S(1)} %copy.25, s32[1536]{0:T(1024)S(1)} %reshape.131), kind=kCustom, calls=%fused_computation.3 | custom fusion | bytes 3158016 | tf_op jit(solution)/shard_map/gather | solution.py:24
  419.9 7.5 multiply_reduce_fusion.1
  430.2 4.0 collective-permute-start.14
  434.2 3.4 collective-permute-start.13
  439.8 65.1 %psum.45 = f32[256]{0:T(256)S(1)} all-reduce(f32[256]{0:T(256)S(1)} %broadcast_multiply_fusion.1), channel_id=1, replica_groups=mesh['sx'=8,'sy'=16] {'sx','sy'}, use_global_device_ids=true, to_apply=%region_6.0 | all-reduce | flops 256 | bytes 2048 | tf_op jit(solution)/shard_map/psum | solution.py:56
  509.3 17.9 %gather_fusion.4 = f32[1536,256]{1,0:T(8,128)} fusion(f32[4,384,256]{2,1,0:T(8,128)S(1)} %copy.27, s32[1536]{0:T(1024)S(1)} %reshape.131), kind=kCustom, calls=%fused_computation.4 | custom fusion | bytes 3158016 | tf_op jit(solution)/shard_map/gather | solution.py:24
  534.4 7.7 fusion
  542.2 134.3 %all-reduce.8.cloned.1.call-done = f32[512,256]{1,0:T(8,128)} async-done(((f32[512,256]{1,0:T(8,128)}), f32[512,256]{1,0:T(8,128)}) %all-reduce.8.cloned.1.call-update) | async-done | bytes 524304 | tf_op jit(solution)/shard_map/psum | solution.py:30
  677.9 54.1 %all-gather.1 = f32[128,4,256]{2,1,0:T(4,128)} all-gather(f32[1,4,256]{2,1,0:T(4,128)S(1)} %convolution_bitcast_fusion), channel_id=1, replica_groups=mesh['sx'=8,'sy'=16] {'sx','sy'}, dimensions={0}, use_global_device_ids=true | all-gather | bytes 528384 | tf_op jit(solution)/shard_map/all_gather | solution.py:32
  742.7 4.0 collective-permute-start.18
  752.3 65.2 %psum.47 = f32[256]{0:T(256)S(1)} all-reduce(f32[256]{0:T(256)S(1)} %get-tuple-element.38), channel_id=1, replica_groups=mesh['sx'=8,'sy'=16] {'sx','sy'}, use_global_device_ids=true, to_apply=%region_9.0 | all-reduce | flops 256 | bytes 2048 | tf_op jit(solution)/shard_map/psum | solution.py:56
  821.8 17.9 %gather_fusion.6 = f32[1536,256]{1,0:T(8,128)} fusion(f32[4,384,256]{2,1,0:T(8,128)S(1)} %copy.29, s32[1536]{0:T(1024)S(1)} %reshape.131), kind=kCustom, calls=%fused_computation.6 | custom fusion | bytes 3158016 | tf_op jit(solution)/shard_map/gather | solution.py:24
  842.9 4.8 subtract_bitcast_fusion
  (125 shorter events, 110.8 us)
Async XLA Ops:
  7.2 245.1 %all-reduce.6.cloned.1.call-start = ((), (), s32[]{:S(2)}) async-start(), calls=%async_computation | async-start | bytes 1048576 | tf_op jit(solution)/shard_map/psum | solution.py:30
  8.7 13.2 %collective-permute-start.3 = (f32[384,256]{1,0:T(8,128)S(1)}, f32[384,256]{1,0:T(8,128)S(1)}, u32[]{:S(2)}, u32[]{:S(2)}) collective-permute-start(f32[384,256]{1,0:T(8,128)S(1)} %get-tuple-element.29), channel_id=1, source_target_pairs={{1,0},{2,1},{3,2},{4,3},{5,4},{6,5},{7,6},{8,7},{9,8},{10,9},{11,1... | collective-permute-start | bytes 1179656 | tf_op jit(solution)/shard_map/ppermute | solution.py:12
  10.0 12.8 %collective-permute-start.2 = (f32[384,256]{1,0:T(8,128)S(1)}, f32[384,256]{1,0:T(8,128)S(1)}, u32[]{:S(2)}, u32[]{:S(2)}) collective-permute-start(f32[384,256]{1,0:T(8,128)S(1)} %get-tuple-element.30), channel_id=1, source_target_pairs={{0,1},{1,2},{2,3},{3,4},{4,5},{5,6},{6,7},{7,8},{8,9},{9,10},{10,1... | collective-permute-start | bytes 1179656 | tf_op jit(solution)/shard_map/ppermute | solution.py:12
  15.0 9.6 %collective-permute-start.1 = (f32[384,256]{1,0:T(8,128)S(1)}, f32[384,256]{1,0:T(8,128)S(1)}, u32[]{:S(2)}, u32[]{:S(2)}) collective-permute-start(f32[384,256]{1,0:T(8,128)S(1)} %get-tuple-element.31), channel_id=1, source_target_pairs={{16,0},{32,16},{48,32},{64,48},{80,64},{96,80},{112,96},{17,1},{33... | collective-permute-start | bytes 1179656 | tf_op jit(solution)/shard_map/ppermute | solution.py:12
  17.9 7.9 collective-permute-start
  52.1 16.6 %collective-permute-start.7 = (f32[384,256]{0,1:T(8,128)}, f32[384,256]{0,1:T(8,128)}, u32[]{:S(2)}, u32[]{:S(2)}) collective-permute-start(f32[384,256]{0,1:T(8,128)} %get-tuple-element.25), channel_id=1, source_target_pairs={{1,0},{2,1},{3,2},{4,3},{5,4},{6,5},{7,6},{8,7},{9,8},{10,9},{11,1... | collective-permute-start | bytes 1179656 | tf_op jit(solution)/shard_map/ppermute | solution.py:12
  53.4 15.3 %collective-permute-start.6 = (f32[384,256]{0,1:T(8,128)}, f32[384,256]{0,1:T(8,128)}, u32[]{:S(2)}, u32[]{:S(2)}) collective-permute-start(f32[384,256]{0,1:T(8,128)} %get-tuple-element.26), channel_id=1, source_target_pairs={{0,1},{1,2},{2,3},{3,4},{4,5},{5,6},{6,7},{7,8},{8,9},{9,10},{10,1... | collective-permute-start | bytes 1179656 | tf_op jit(solution)/shard_map/ppermute | solution.py:12
  58.3 10.5 %collective-permute-start.5 = (f32[384,256]{0,1:T(8,128)}, f32[384,256]{0,1:T(8,128)}, u32[]{:S(2)}, u32[]{:S(2)}) collective-permute-start(f32[384,256]{0,1:T(8,128)} %get-tuple-element.27), channel_id=1, source_target_pairs={{16,0},{32,16},{48,32},{64,48},{80,64},{96,80},{112,96},{17,1},{33... | collective-permute-start | bytes 1179656 | tf_op jit(solution)/shard_map/ppermute | solution.py:12
  60.2 9.8 %collective-permute-start.4 = (f32[384,256]{0,1:T(8,128)}, f32[384,256]{0,1:T(8,128)}, u32[]{:S(2)}, u32[]{:S(2)}) collective-permute-start(f32[384,256]{0,1:T(8,128)} %get-tuple-element.24), channel_id=1, source_target_pairs={{0,16},{16,32},{32,48},{48,64},{64,80},{80,96},{96,112},{1,17},{17... | collective-permute-start | bytes 1179656 | tf_op jit(solution)/shard_map/ppermute | solution.py:12
  100.4 151.9 %copy-start.15 = (f32[4,512]{1,0:T(4,128)S(1)}, f32[4,512]{1,0:T(4,128)}, u32[]{:S(2)}) copy-start(f32[4,512]{1,0:T(4,128)} %param.13) | copy-start | bytes 24580
  100.4 576.1 %all-reduce.8.cloned.1.call-start = ((), (), s32[]{:S(2)}) async-start(), calls=%async_computation.1 | async-start | bytes 1048576 | tf_op jit(solution)/shard_map/psum | solution.py:30
  315.9 75.8 %collective-permute-start.11 = (f32[384,256]{0,1:T(8,128)}, f32[384,256]{0,1:T(8,128)S(1)}, u32[]{:S(2)}, u32[]{:S(2)}) collective-permute-start(f32[384,256]{0,1:T(8,128)} %get-tuple-element.21), channel_id=1, source_target_pairs={{1,0},{2,1},{3,2},{4,3},{5,4},{6,5},{7,6},{8,7},{9,8},{10,9},{11,1... | collective-permute-start | bytes 1179656 | tf_op jit(solution)/shard_map/ppermute | solution.py:12
  317.2 74.5 %collective-permute-start.10 = (f32[384,256]{0,1:T(8,128)}, f32[384,256]{0,1:T(8,128)S(1)}, u32[]{:S(2)}, u32[]{:S(2)}) collective-permute-start(f32[384,256]{0,1:T(8,128)} %get-tuple-element.22), channel_id=1, source_target_pairs={{0,1},{1,2},{2,3},{3,4},{4,5},{5,6},{6,7},{7,8},{8,9},{9,10},{10,1... | collective-permute-start | bytes 1179656 | tf_op jit(solution)/shard_map/ppermute | solution.py:12
  321.2 70.5 %collective-permute-start.9 = (f32[384,256]{0,1:T(8,128)S(1)}, f32[384,256]{0,1:T(8,128)}, u32[]{:S(2)}, u32[]{:S(2)}) collective-permute-start(f32[384,256]{0,1:T(8,128)S(1)} %get-tuple-element.23), channel_id=1, source_target_pairs={{16,0},{32,16},{48,32},{64,48},{80,64},{96,80},{112,96},{17,1},{33... | collective-permute-start | bytes 1179656 | tf_op jit(solution)/shard_map/ppermute | solution.py:12
  323.7 68.0 %collective-permute-start.8 = (f32[384,256]{0,1:T(8,128)S(1)}, f32[384,256]{0,1:T(8,128)}, u32[]{:S(2)}, u32[]{:S(2)}) collective-permute-start(f32[384,256]{0,1:T(8,128)S(1)} %get-tuple-element.20), channel_id=1, source_target_pairs={{0,16},{16,32},{32,48},{48,64},{64,80},{80,96},{96,112},{1,17},{17... | collective-permute-start | bytes 1179656 | tf_op jit(solution)/shard_map/ppermute | solution.py:12
  428.9 76.0 %collective-permute-start.15 = (f32[384,256]{0,1:T(8,128)}, f32[384,256]{0,1:T(8,128)S(1)}, u32[]{:S(2)}, u32[]{:S(2)}) collective-permute-start(f32[384,256]{0,1:T(8,128)} %get-tuple-element.15), channel_id=1, source_target_pairs={{1,0},{2,1},{3,2},{4,3},{5,4},{6,5},{7,6},{8,7},{9,8},{10,9},{11,1... | collective-permute-start | bytes 1179656 | tf_op jit(solution)/shard_map/ppermute | solution.py:12
  430.2 74.7 %collective-permute-start.14 = (f32[384,256]{0,1:T(8,128)}, f32[384,256]{0,1:T(8,128)S(1)}, u32[]{:S(2)}, u32[]{:S(2)}) collective-permute-start(f32[384,256]{0,1:T(8,128)} %get-tuple-element.16), channel_id=1, source_target_pairs={{0,1},{1,2},{2,3},{3,4},{4,5},{5,6},{6,7},{7,8},{8,9},{9,10},{10,1... | collective-permute-start | bytes 1179656 | tf_op jit(solution)/shard_map/ppermute | solution.py:12
  434.2 70.7 %collective-permute-start.13 = (f32[384,256]{0,1:T(8,128)S(1)}, f32[384,256]{0,1:T(8,128)}, u32[]{:S(2)}, u32[]{:S(2)}) collective-permute-start(f32[384,256]{0,1:T(8,128)S(1)} %get-tuple-element.17), channel_id=1, source_target_pairs={{16,0},{32,16},{48,32},{64,48},{80,64},{96,80},{112,96},{17,1},{33... | collective-permute-start | bytes 1179656 | tf_op jit(solution)/shard_map/ppermute | solution.py:12
  437.6 67.3 %collective-permute-start.12 = (f32[384,256]{0,1:T(8,128)S(1)}, f32[384,256]{0,1:T(8,128)}, u32[]{:S(2)}, u32[]{:S(2)}) collective-permute-start(f32[384,256]{0,1:T(8,128)S(1)} %get-tuple-element.14), channel_id=1, source_target_pairs={{0,16},{16,32},{32,48},{48,64},{64,80},{80,96},{96,112},{1,17},{17... | collective-permute-start | bytes 1179656 | tf_op jit(solution)/shard_map/ppermute | solution.py:12
  532.4 205.1 %copy-start.1 = (f32[1536,256]{0,1:T(8,128)}, f32[1536,256]{0,1:T(8,128)S(1)}, u32[]{:S(2)}) copy-start(f32[1536,256]{0,1:T(8,128)S(1)} %multiply_add_fusion) | copy-start | bytes 4718596
  741.4 76.0 %collective-permute-start.19 = (f32[384,256]{0,1:T(8,128)}, f32[384,256]{0,1:T(8,128)S(1)}, u32[]{:S(2)}, u32[]{:S(2)}) collective-permute-start(f32[384,256]{0,1:T(8,128)} %get-tuple-element.11), channel_id=1, source_target_pairs={{1,0},{2,1},{3,2},{4,3},{5,4},{6,5},{7,6},{8,7},{9,8},{10,9},{11,1... | collective-permute-start | bytes 1179656 | tf_op jit(solution)/shard_map/ppermute | solution.py:12
  742.7 74.8 %collective-permute-start.18 = (f32[384,256]{0,1:T(8,128)}, f32[384,256]{0,1:T(8,128)S(1)}, u32[]{:S(2)}, u32[]{:S(2)}) collective-permute-start(f32[384,256]{0,1:T(8,128)} %get-tuple-element.12), channel_id=1, source_target_pairs={{0,1},{1,2},{2,3},{3,4},{4,5},{5,6},{6,7},{7,8},{8,9},{9,10},{10,1... | collective-permute-start | bytes 1179656 | tf_op jit(solution)/shard_map/ppermute | solution.py:12
  746.7 70.7 %collective-permute-start.17 = (f32[384,256]{0,1:T(8,128)S(1)}, f32[384,256]{0,1:T(8,128)}, u32[]{:S(2)}, u32[]{:S(2)}) collective-permute-start(f32[384,256]{0,1:T(8,128)S(1)} %get-tuple-element.13), channel_id=1, source_target_pairs={{16,0},{32,16},{48,32},{64,48},{80,64},{96,80},{112,96},{17,1},{33... | collective-permute-start | bytes 1179656 | tf_op jit(solution)/shard_map/ppermute | solution.py:12
  749.2 68.3 %collective-permute-start.16 = (f32[384,256]{0,1:T(8,128)S(1)}, f32[384,256]{0,1:T(8,128)}, u32[]{:S(2)}, u32[]{:S(2)}) collective-permute-start(f32[384,256]{0,1:T(8,128)S(1)} %get-tuple-element.10), channel_id=1, source_target_pairs={{0,16},{16,32},{32,48},{48,64},{64,80},{80,96},{96,112},{1,17},{17... | collective-permute-start | bytes 1179656 | tf_op jit(solution)/shard_map/ppermute | solution.py:12
  (16 other events, 186.9 us)
Sparse Core Ops, SparseCore 0:
  100.5 151.7 all-reduce.5
  534.6 141.8 all-reduce.7
where the time goes:
time: 861 us; the launch traced here: 859 us
  blocking collectives  303 us (35%)
  waiting for transfers between devices  285 us (33%)
  local copies, waits for them, and re-layouts  130 us (15%)
  starting transfers between devices  58.1 us (7%)
  matrix products  44.1 us (5%)
  other arithmetic  24 us (3%)
  between operations  14.6 us (2%)
    psum x2, waiting for transfers between devices, coarse_solve(): total = lax.psum(coarse_rhs, ('sx', 'sy'))  279 us
    psum x3, blocking collectives, total(): return lax.psum(values, ('sx', 'sy'))  195 us
    all_gather x2, blocking collectives, coarse_solve(): return lax.all_gather(mine, ('sx', 'sy'), axis=0, tiled=True)  108 us
    gather x10, local copies, waits for them, and re-layouts, jump(): matched = received[jnp.arange(4, dtype=jnp.int32)[:, None], face_index]  96.4 us
    ppermute x20, starting transfers between devices, shifted(): return lax.ppermute(block, axis, route)  57.8 us
    dot_general x2, matrix products, shards(): operator_applied = jnp.dot(prec_mat, spread, precision=high)  19.4 us
  transfers between devices with their start and end apart: 22, of which 8 were waited for; matrix products, arithmetic and copies ran while one was open for 2% of the time, Pallas kernels for 0%

commit v1 on v0

--- a/solution.py
+++ b/solution.py
@@ -53,7 +53,7 @@
     scale = jnp.repeat(1.0 + inside.astype(jnp.float32), size)[:, None]
 
     def total(values):
-        return lax.psum(values, ("sx", "sy"))
+        return lax.psum(lax.psum(values, "sx"), "sy")
 
     residual = jump(loads[0, 0], face_index)
     multipliers = jnp.zeros_like(residual)

time: 861 us -> 808 us (0.938)
  blocking collectives: 303 us -> 232 us
    psum x3 -> x6, blocking collectives: 195 us -> 124 us  [total(): return lax.psum(lax.psum(values, 'sx'), 'sy')]
where the time goes in v1:
time: 808 us; the launch traced here: 800 us
  waiting for transfers between devices  289 us (36%)
  blocking collectives  232 us (29%)
  local copies, waits for them, and re-layouts  130 us (16%)
  starting transfers between devices  65.8 us (8%)
  matrix products  44.1 us (5%)
  other arithmetic  24 us (3%)
  between operations  14.6 us (2%)
    psum x2, waiting for transfers between devices, coarse_solve(): total = lax.psum(coarse_rhs, ('sx', 'sy'))  283 us
    psum x6, blocking collectives, total(): return lax.psum(lax.psum(values, 'sx'), 'sy')  124 us
    all_gather x2, blocking collectives, coarse_solve(): return lax.all_gather(mine, ('sx', 'sy'), axis=0, tiled=True)  108 us
    gather x10, local copies, waits for them, and re-layouts, jump(): matched = received[jnp.arange(4, dtype=jnp.int32)[:, None], face_index]  96.3 us
    ppermute x20, starting transfers between devices, shifted(): return lax.ppermute(block, axis, route)  65.5 us
    dot_general x2, matrix products, shards(): operator_applied = jnp.dot(prec_mat, spread, precision=high)  19.4 us
  transfers between devices with their start and end apart: 22, of which 8 were waited for; matrix products, arithmetic and copies ran while one was open for 2% of the time, Pallas kernels for 0%

profile of v1, /device:TPU:1, one launch (start us, length us, event | category | flops | bytes accessed | tf_op | source)
XLA Modules:
  0.0 799.6 jit_solution(2014983860255474838)
XLA Ops:
  10.0 5.0 collective-permute-start.2
  27.9 10.7 %gather_fusion = f32[1536,256]{1,0:T(8,128)S(1)} fusion(f32[4,384,256]{2,1,0:T(8,128)S(1)} %pad_maximum_fusion, s32[1536]{0:T(1024)S(1)} %reshape.131), kind=kCustom, calls=%fused_computation | custom fusion | bytes 3158016 | tf_op jit(solution)/shard_map/gather | solution.py:24
  38.6 11.8 %fusion.10 = f32[1536,256]{0,1:T(8,128)S(1)} fusion(f32[1,1,1536,1536]{3,2,1,0:T(8,128)} %param.9, f32[1,1,1536,256]{3,2,1,0:T(8,128)} %param.7, f32[1536,256]{1,0:T(8,128)S(1)} %gather_fusion, f32[1536]{0:T(1024)S(1)} %mul.105), kind=kOutput, calls=%fused_computation.19 | convolution fusion | flops 3624665088 | bytes 14161920 | tf_op jit(solution)/shard_map/dot_general | solution.py:64
  53.4 4.9 collective-permute-start.6
  60.2 4.8 collective-permute-start.4
  74.5 17.9 %gather_fusion.1 = f32[1536,256]{1,0:T(8,128)} fusion(f32[4,384,256]{2,1,0:T(8,128)S(1)} %copy.21, s32[1536]{0:T(1024)S(1)} %reshape.131), kind=kCustom, calls=%fused_computation.1 | custom fusion | bytes 3158016 | tf_op jit(solution)/shard_map/gather | solution.py:24
  100.6 6.7 fusion.2
  107.4 144.9 %all-reduce.7.cloned.1.call-done = f32[512,256]{1,0:T(8,128)} async-done(((f32[512,256]{1,0:T(8,128)}), f32[512,256]{1,0:T(8,128)}) %all-reduce.7.cloned.1.call-update) | async-done | bytes 524304 | tf_op jit(solution)/shard_map/psum | solution.py:30
  253.6 54.1 %all-gather = f32[128,4,256]{2,1,0:T(4,128)} all-gather(f32[1,4,256]{2,1,0:T(4,128)S(1)} %convolution_bitcast_fusion.1), channel_id=1, replica_groups=mesh['sx'=8,'sy'=16] {'sx','sy'}, dimensions={0}, use_global_device_ids=true | all-gather | bytes 528384 | tf_op jit(solution)/shard_map/all_gather | solution.py:32
  326.7 11.8 %all-reduce.3 = (f32[256]{0:T(256)S(1)}, f32[256]{0:T(256)S(1)}) all-reduce(f32[256]{0:T(256)S(1)} %broadcast_multiply_fusion.3, f32[256]{0:T(256)S(1)} %get-tuple-element.36), channel_id=1, replica_groups=mesh['sx'=8,'sy'=16] {'sx'}, use_global_device_ids=true, to_apply=%region_1.0 | all-reduce | flops 512 | bytes 4096 | tf_op jit(solution)/shard_map/psum | solution.py:56
  338.5 28.6 %all-reduce.2 = (f32[256]{0:T(256)S(1)}, f32[256]{0:T(256)S(1)}) all-reduce(f32[256]{0:T(256)S(1)} %get-tuple-element.8, f32[256]{0:T(256)S(1)} %get-tuple-element.9), channel_id=1, replica_groups=mesh['sx'=8,'sy'=16] {'sy'}, use_global_device_ids=true, to_apply=%region_2.0 | all-reduce | flops 512 | bytes 4096 | tf_op jit(solution)/shard_map/psum | solution.py:56
  371.4 17.9 %gather_fusion.3 = f32[1536,256]{1,0:T(8,128)} fusion(f32[4,384,256]{2,1,0:T(8,128)S(1)} %copy.25, s32[1536]{0:T(1024)S(1)} %reshape.131), kind=kCustom, calls=%fused_computation.3 | custom fusion | bytes 3158016 | tf_op jit(solution)/shard_map/gather | solution.py:24
  395.3 7.5 multiply_reduce_fusion.1
  409.7 11.2 %collective-permute-start.13 = (f32[384,256]{0,1:T(8,128)S(1)}, f32[384,256]{0,1:T(8,128)}, u32[]{:S(2)}, u32[]{:S(2)}) collective-permute-start(f32[384,256]{0,1:T(8,128)S(1)} %get-tuple-element.19), channel_id=1, source_target_pairs={{16,0},{32,16},{48,32},{64,48},{80,64},{96,80},{112,96},{17,1},{33... | collective-permute-start | bytes 1179656 | tf_op jit(solution)/shard_map/ppermute | solution.py:12
  422.9 13.0 %psum.75 = f32[256]{0:T(256)S(1)} all-reduce(f32[256]{0:T(256)S(1)} %broadcast_multiply_fusion.1), channel_id=1, replica_groups=mesh['sx'=8,'sy'=16] {'sx'}, use_global_device_ids=true, to_apply=%region_8.0 | all-reduce | flops 256 | bytes 2048 | tf_op jit(solution)/shard_map/psum | solution.py:56
  435.9 30.0 %psum.76 = f32[256]{0:T(256)S(1)} all-reduce(f32[256]{0:T(256)S(1)} %psum.75), channel_id=1, replica_groups=mesh['sx'=8,'sy'=16] {'sy'}, use_global_device_ids=true, to_apply=%region_9.0 | all-reduce | flops 256 | bytes 2048 | tf_op jit(solution)/shard_map/psum | solution.py:56
  470.2 17.9 %gather_fusion.4 = f32[1536,256]{1,0:T(8,128)} fusion(f32[4,384,256]{2,1,0:T(8,128)S(1)} %copy.27, s32[1536]{0:T(1024)S(1)} %reshape.131), kind=kCustom, calls=%fused_computation.4 | custom fusion | bytes 3158016 | tf_op jit(solution)/shard_map/gather | solution.py:24
  495.3 7.7 fusion
  503.0 138.6 %all-reduce.9.cloned.1.call-done = f32[512,256]{1,0:T(8,128)} async-done(((f32[512,256]{1,0:T(8,128)}), f32[512,256]{1,0:T(8,128)}) %all-reduce.9.cloned.1.call-update) | async-done | bytes 524304 | tf_op jit(solution)/shard_map/psum | solution.py:30
  643.0 54.1 %all-gather.1 = f32[128,4,256]{2,1,0:T(4,128)} all-gather(f32[1,4,256]{2,1,0:T(4,128)S(1)} %convolution_bitcast_fusion), channel_id=1, replica_groups=mesh['sx'=8,'sy'=16] {'sx','sy'}, dimensions={0}, use_global_device_ids=true | all-gather | bytes 528384 | tf_op jit(solution)/shard_map/all_gather | solution.py:32
  717.5 11.8 %psum.78 = f32[256]{0:T(256)S(1)} all-reduce(f32[256]{0:T(256)S(1)} %get-tuple-element.40), channel_id=1, replica_groups=mesh['sx'=8,'sy'=16] {'sx'}, use_global_device_ids=true, to_apply=%region_12.0 | all-reduce | flops 256 | bytes 2048 | tf_op jit(solution)/shard_map/psum | solution.py:56
  729.3 28.6 %psum.79 = f32[256]{0:T(256)S(1)} all-reduce(f32[256]{0:T(256)S(1)} %psum.78), channel_id=1, replica_groups=mesh['sx'=8,'sy'=16] {'sy'}, use_global_device_ids=true, to_apply=%region_13.0 | all-reduce | flops 256 | bytes 2048 | tf_op jit(solution)/shard_map/psum | solution.py:56
  762.2 17.9 %gather_fusion.6 = f32[1536,256]{1,0:T(8,128)} fusion(f32[4,384,256]{2,1,0:T(8,128)S(1)} %copy.29, s32[1536]{0:T(1024)S(1)} %reshape.131), kind=kCustom, calls=%fused_computation.6 | custom fusion | bytes 3158016 | tf_op jit(solution)/shard_map/gather | solution.py:24
  783.2 4.7 subtract_bitcast_fusion
  (128 shorter events, 122.5 us)
Async XLA Ops:
  7.2 245.1 %all-reduce.7.cloned.1.call-start = ((), (), s32[]{:S(2)}) async-start(), calls=%async_computation | async-start | bytes 1048576 | tf_op jit(solution)/shard_map/psum | solution.py:30
  8.7 13.2 %collective-permute-start.3 = (f32[384,256]{1,0:T(8,128)S(1)}, f32[384,256]{1,0:T(8,128)S(1)}, u32[]{:S(2)}, u32[]{:S(2)}) collective-permute-start(f32[384,256]{1,0:T(8,128)S(1)} %get-tuple-element.31), channel_id=1, source_target_pairs={{1,0},{2,1},{3,2},{4,3},{5,4},{6,5},{7,6},{8,7},{9,8},{10,9},{11,1... | collective-permute-start | bytes 1179656 | tf_op jit(solution)/shard_map/ppermute | solution.py:12
  10.0 12.8 %collective-permute-start.2 = (f32[384,256]{1,0:T(8,128)S(1)}, f32[384,256]{1,0:T(8,128)S(1)}, u32[]{:S(2)}, u32[]{:S(2)}) collective-permute-start(f32[384,256]{1,0:T(8,128)S(1)} %get-tuple-element.32), channel_id=1, source_target_pairs={{0,1},{1,2},{2,3},{3,4},{4,5},{5,6},{6,7},{7,8},{8,9},{9,10},{10,1... | collective-permute-start | bytes 1179656 | tf_op jit(solution)/shard_map/ppermute | solution.py:12
  15.0 9.6 %collective-permute-start.1 = (f32[384,256]{1,0:T(8,128)S(1)}, f32[384,256]{1,0:T(8,128)S(1)}, u32[]{:S(2)}, u32[]{:S(2)}) collective-permute-start(f32[384,256]{1,0:T(8,128)S(1)} %get-tuple-element.33), channel_id=1, source_target_pairs={{16,0},{32,16},{48,32},{64,48},{80,64},{96,80},{112,96},{17,1},{33... | collective-permute-start | bytes 1179656 | tf_op jit(solution)/shard_map/ppermute | solution.py:12
  17.9 7.9 collective-permute-start
  52.1 16.6 %collective-permute-start.7 = (f32[384,256]{0,1:T(8,128)}, f32[384,256]{0,1:T(8,128)}, u32[]{:S(2)}, u32[]{:S(2)}) collective-permute-start(f32[384,256]{0,1:T(8,128)} %get-tuple-element.27), channel_id=1, source_target_pairs={{1,0},{2,1},{3,2},{4,3},{5,4},{6,5},{7,6},{8,7},{9,8},{10,9},{11,1... | collective-permute-start | bytes 1179656 | tf_op jit(solution)/shard_map/ppermute | solution.py:12
  53.4 15.3 %collective-permute-start.6 = (f32[384,256]{0,1:T(8,128)}, f32[384,256]{0,1:T(8,128)}, u32[]{:S(2)}, u32[]{:S(2)}) collective-permute-start(f32[384,256]{0,1:T(8,128)} %get-tuple-element.28), channel_id=1, source_target_pairs={{0,1},{1,2},{2,3},{3,4},{4,5},{5,6},{6,7},{7,8},{8,9},{9,10},{10,1... | collective-permute-start | bytes 1179656 | tf_op jit(solution)/shard_map/ppermute | solution.py:12
  58.3 10.5 %collective-permute-start.5 = (f32[384,256]{0,1:T(8,128)}, f32[384,256]{0,1:T(8,128)}, u32[]{:S(2)}, u32[]{:S(2)}) collective-permute-start(f32[384,256]{0,1:T(8,128)} %get-tuple-element.29), channel_id=1, source_target_pairs={{16,0},{32,16},{48,32},{64,48},{80,64},{96,80},{112,96},{17,1},{33... | collective-permute-start | bytes 1179656 | tf_op jit(solution)/shard_map/ppermute | solution.py:12
  60.2 9.8 %collective-permute-start.4 = (f32[384,256]{0,1:T(8,128)}, f32[384,256]{0,1:T(8,128)}, u32[]{:S(2)}, u32[]{:S(2)}) collective-permute-start(f32[384,256]{0,1:T(8,128)} %get-tuple-element.26), channel_id=1, source_target_pairs={{0,16},{16,32},{32,48},{48,64},{64,80},{80,96},{96,112},{1,17},{17... | collective-permute-start | bytes 1179656 | tf_op jit(solution)/shard_map/ppermute | solution.py:12
  100.4 151.9 %copy-start.15 = (f32[4,512]{1,0:T(4,128)S(1)}, f32[4,512]{1,0:T(4,128)}, u32[]{:S(2)}) copy-start(f32[4,512]{1,0:T(4,128)} %param.13) | copy-start | bytes 24580
  100.4 541.2 %all-reduce.9.cloned.1.call-start = ((), (), s32[]{:S(2)}) async-start(), calls=%async_computation.1 | async-start | bytes 1048576 | tf_op jit(solution)/shard_map/psum | solution.py:30
  315.8 51.3 %collective-permute-start.11 = (f32[384,256]{0,1:T(8,128)}, f32[384,256]{0,1:T(8,128)S(1)}, u32[]{:S(2)}, u32[]{:S(2)}) collective-permute-start(f32[384,256]{0,1:T(8,128)} %get-tuple-element.23), channel_id=1, source_target_pairs={{1,0},{2,1},{3,2},{4,3},{5,4},{6,5},{7,6},{8,7},{9,8},{10,9},{11,1... | collective-permute-start | bytes 1179656 | tf_op jit(solution)/shard_map/ppermute | solution.py:12
  317.1 50.0 %collective-permute-start.10 = (f32[384,256]{0,1:T(8,128)}, f32[384,256]{0,1:T(8,128)S(1)}, u32[]{:S(2)}, u32[]{:S(2)}) collective-permute-start(f32[384,256]{0,1:T(8,128)} %get-tuple-element.24), channel_id=1, source_target_pairs={{0,1},{1,2},{2,3},{3,4},{4,5},{5,6},{6,7},{7,8},{8,9},{9,10},{10,1... | collective-permute-start | bytes 1179656 | tf_op jit(solution)/shard_map/ppermute | solution.py:12
  321.1 46.0 %collective-permute-start.9 = (f32[384,256]{0,1:T(8,128)S(1)}, f32[384,256]{0,1:T(8,128)}, u32[]{:S(2)}, u32[]{:S(2)}) collective-permute-start(f32[384,256]{0,1:T(8,128)S(1)} %get-tuple-element.25), channel_id=1, source_target_pairs={{16,0},{32,16},{48,32},{64,48},{80,64},{96,80},{112,96},{17,1},{33... | collective-permute-start | bytes 1179656 | tf_op jit(solution)/shard_map/ppermute | solution.py:12
  323.6 43.5 %collective-permute-start.8 = (f32[384,256]{0,1:T(8,128)S(1)}, f32[384,256]{0,1:T(8,128)}, u32[]{:S(2)}, u32[]{:S(2)}) collective-permute-start(f32[384,256]{0,1:T(8,128)S(1)} %get-tuple-element.22), channel_id=1, source_target_pairs={{0,16},{16,32},{32,48},{48,64},{64,80},{80,96},{96,112},{1,17},{17... | collective-permute-start | bytes 1179656 | tf_op jit(solution)/shard_map/ppermute | solution.py:12
  404.3 61.5 %collective-permute-start.15 = (f32[384,256]{0,1:T(8,128)}, f32[384,256]{0,1:T(8,128)S(1)}, u32[]{:S(2)}, u32[]{:S(2)}) collective-permute-start(f32[384,256]{0,1:T(8,128)} %get-tuple-element.17), channel_id=1, source_target_pairs={{1,0},{2,1},{3,2},{4,3},{5,4},{6,5},{7,6},{8,7},{9,8},{10,9},{11,1... | collective-permute-start | bytes 1179656 | tf_op jit(solution)/shard_map/ppermute | solution.py:12
  405.6 60.3 %collective-permute-start.14 = (f32[384,256]{0,1:T(8,128)}, f32[384,256]{0,1:T(8,128)S(1)}, u32[]{:S(2)}, u32[]{:S(2)}) collective-permute-start(f32[384,256]{0,1:T(8,128)} %get-tuple-element.18), channel_id=1, source_target_pairs={{0,1},{1,2},{2,3},{3,4},{4,5},{5,6},{6,7},{7,8},{8,9},{9,10},{10,1... | collective-permute-start | bytes 1179656 | tf_op jit(solution)/shard_map/ppermute | solution.py:12
  409.7 56.2 %collective-permute-start.13 = (f32[384,256]{0,1:T(8,128)S(1)}, f32[384,256]{0,1:T(8,128)}, u32[]{:S(2)}, u32[]{:S(2)}) collective-permute-start(f32[384,256]{0,1:T(8,128)S(1)} %get-tuple-element.19), channel_id=1, source_target_pairs={{16,0},{32,16},{48,32},{64,48},{80,64},{96,80},{112,96},{17,1},{33... | collective-permute-start | bytes 1179656 | tf_op jit(solution)/shard_map/ppermute | solution.py:12
  421.0 44.9 %collective-permute-start.12 = (f32[384,256]{0,1:T(8,128)S(1)}, f32[384,256]{0,1:T(8,128)}, u32[]{:S(2)}, u32[]{:S(2)}) collective-permute-start(f32[384,256]{0,1:T(8,128)S(1)} %get-tuple-element.16), channel_id=1, source_target_pairs={{0,16},{16,32},{32,48},{48,64},{64,80},{80,96},{96,112},{1,17},{17... | collective-permute-start | bytes 1179656 | tf_op jit(solution)/shard_map/ppermute | solution.py:12
  493.3 209.3 %copy-start.1 = (f32[1536,256]{0,1:T(8,128)}, f32[1536,256]{0,1:T(8,128)S(1)}, u32[]{:S(2)}) copy-start(f32[1536,256]{0,1:T(8,128)S(1)} %multiply_add_fusion) | copy-start | bytes 4718596
  706.6 51.3 %collective-permute-start.19 = (f32[384,256]{0,1:T(8,128)}, f32[384,256]{0,1:T(8,128)S(1)}, u32[]{:S(2)}, u32[]{:S(2)}) collective-permute-start(f32[384,256]{0,1:T(8,128)} %get-tuple-element.13), channel_id=1, source_target_pairs={{1,0},{2,1},{3,2},{4,3},{5,4},{6,5},{7,6},{8,7},{9,8},{10,9},{11,1... | collective-permute-start | bytes 1179656 | tf_op jit(solution)/shard_map/ppermute | solution.py:12
  707.9 50.0 %collective-permute-start.18 = (f32[384,256]{0,1:T(8,128)}, f32[384,256]{0,1:T(8,128)S(1)}, u32[]{:S(2)}, u32[]{:S(2)}) collective-permute-start(f32[384,256]{0,1:T(8,128)} %get-tuple-element.14), channel_id=1, source_target_pairs={{0,1},{1,2},{2,3},{3,4},{4,5},{5,6},{6,7},{7,8},{8,9},{9,10},{10,1... | collective-permute-start | bytes 1179656 | tf_op jit(solution)/shard_map/ppermute | solution.py:12
  711.9 46.0 %collective-permute-start.17 = (f32[384,256]{0,1:T(8,128)S(1)}, f32[384,256]{0,1:T(8,128)}, u32[]{:S(2)}, u32[]{:S(2)}) collective-permute-start(f32[384,256]{0,1:T(8,128)S(1)} %get-tuple-element.15), channel_id=1, source_target_pairs={{16,0},{32,16},{48,32},{64,48},{80,64},{96,80},{112,96},{17,1},{33... | collective-permute-start | bytes 1179656 | tf_op jit(solution)/shard_map/ppermute | solution.py:12
  714.3 43.5 %collective-permute-start.16 = (f32[384,256]{0,1:T(8,128)S(1)}, f32[384,256]{0,1:T(8,128)}, u32[]{:S(2)}, u32[]{:S(2)}) collective-permute-start(f32[384,256]{0,1:T(8,128)S(1)} %get-tuple-element.12), channel_id=1, source_target_pairs={{0,16},{16,32},{32,48},{48,64},{64,80},{80,96},{96,112},{1,17},{17... | collective-permute-start | bytes 1179656 | tf_op jit(solution)/shard_map/ppermute | solution.py:12
  (16 other events, 186.9 us)
Sparse Core Ops, SparseCore 0:
  100.5 151.6 all-reduce.6
  495.4 146.1 all-reduce.8
